TPU v7x, 32 devices: a whole 2x2x4 slice. The times are simulated.
32 devices in a mesh: band: 8 (over z, core), grid: 4 (over y, x).
Axes of the slice: x: 2, y: 2, z: 4, core: 2. Of those that a mesh axis runs over, the one named last changes fastest.
Arguments:
- orbitals: float32 [8, 128, 128, 128], P('band', 'grid')
- sources: int32 [4], replicated, may hold values from 0 to 7, as said below
Outputs:
- compressed: float32 [8, 128, 128, 128], P(None, 'grid', 'band')
Inputs may be any that keep to these rules, and one draw needn't show every extreme that they name: `sources`: 4 distinct orbital indices in some order.
All inputs are finite; a program needn't handle non-finite values.
Results may differ from a plain program's by a relative error of at most 0.0003.
Values sent between devices are 32-bit elements; how exact they have to be, the bound alone decides.
A program may use at most 64 MiB of HBM per device.

v0:
```python
import functools
import math

import jax
import jax.numpy as jnp
import numpy as np
from jax import lax
from jax.experimental import pallas as pl
from jax.experimental.pallas import tpu as pltpu
from jax.sharding import PartitionSpec as P

highest = lax.Precision.HIGHEST
MESH = pl.DeviceIdType.MESH


def spread_2(block, axis, owner):
    block = jnp.where(lax.axis_index(axis) == owner, block, jnp.zeros_like(block))
    return lax.psum(block, axis)


def cas_table(length):
    index_values = jnp.arange(length, dtype=jnp.int32)
    products = index_values[:, None] * index_values[None, :] % length
    angles = products.astype(jnp.float32) * (2.0 * math.pi / length)
    return jnp.cos(angles) + jnp.sin(angles)


def squared_waves(start, count, length):
    index_values = start + jnp.arange(count, dtype=jnp.int32)
    signed = jnp.where(index_values < length // 2, index_values, index_values - length)
    waves = signed.astype(jnp.float32) * (2.0 * math.pi / length)
    return waves * waves


def general(orbitals, sources):
    band_count, slab_x, full_y, full_z = orbitals.shape
    grid_count = lax.axis_size("grid")
    full_x = slab_x * grid_count
    total_bands = band_count * lax.axis_size("band")
    round_count = sources.shape[0]
    table_x = cas_table(full_x)
    table_y = cas_table(full_y)
    table_z = cas_table(full_z)
    column_y = full_y // grid_count
    start_y = lax.axis_index("grid") * column_y
    waves = (
        squared_waves(0, full_x, full_x)[:, None, None]
        + squared_waves(start_y, column_y, full_y)[None, :, None]
        + squared_waves(0, full_z, full_z)[None, None, :]
    )
    screen = (4.0 * math.pi / full_x) ** 2
    volume = 1.0 / (full_x * full_y * full_z)
    kernel = volume / (waves + screen)

    def plane_transform(field):
        spread = jnp.einsum("bxyz,zk->bxyk", field, table_z, precision=highest)
        return jnp.einsum("bxyk,yj->bxjk", spread, table_y, precision=highest)

    def own_slab(number):
        owner = number // band_count
        local = number % band_count
        return (owner, lax.dynamic_index_in_dim(orbitals, local, 0, keepdims=False))

    def fetch(number):
        owner, slab = own_slab(number)
        return spread_2(slab, "band", owner)

    arrived = [fetch(sources[turn]) for turn in range(round_count)]
    terms = jnp.zeros(orbitals.shape, jnp.float32)
    for turn in range(round_count):
        source = arrived[turn][None]
        spectra = plane_transform(orbitals * source)
        potential_columns = lax.all_to_all(spectra, "grid", split_axis=2, concat_axis=1, tiled=True)
        line_spread = jnp.einsum("bxyz,xa->bayz", potential_columns, table_x, precision=highest)
        line_spread = line_spread * kernel[None]
        filtered = jnp.einsum("bayz,ax->bxyz", line_spread, table_x, precision=highest)
        terms = terms + source * plane_transform(
            lax.all_to_all(filtered, "grid", split_axis=1, concat_axis=2, tiled=True)
        )
    orbital_cols, term_cols = (
        lax.all_to_all(orbitals, "band", split_axis=2, concat_axis=0, tiled=True),
        lax.all_to_all(terms, "band", split_axis=2, concat_axis=0, tiled=True),
    )
    flat_orbitals = orbital_cols.reshape(total_bands, -1)
    flat_terms = term_cols.reshape(total_bands, -1)
    partial_intersection = (
        jnp.dot(flat_orbitals, flat_terms.T, precision=highest, preferred_element_type=jnp.float32)
        * volume
    )
    intersection = lax.psum(partial_intersection, ("band", "grid"))
    factor = jnp.linalg.cholesky(intersection)
    solved = lax.linalg.triangular_solve(factor, flat_terms, left_side=True, lower=True)
    return (-solved).reshape(term_cols.shape)


def parts_of(value):
    high = value.astype(jnp.bfloat16)
    low = (value - high.astype(jnp.float32)).astype(jnp.bfloat16)
    return high, low


def along_rows(left, first, second):
    n = first.shape[0]
    h0, l0 = parts_of(first)
    h1, l1 = parts_of(second)
    right = jnp.concatenate(
        [jnp.concatenate([h0, h1], axis=1), jnp.concatenate([l0, l1], axis=1)], axis=0
    )
    both = jnp.dot(left, right, preferred_element_type=jnp.float32)
    return both[:n] + both[n:]


def along_lanes(rows, right):
    n = rows.shape[1]
    high, low = parts_of(rows)
    both = jnp.dot(
        jnp.concatenate([high, low], axis=1), right, preferred_element_type=jnp.float32
    )
    return both[:, :n] + both[:, n:]


def whole_kernel(
    bands, grids, rounds, chunks, unit, ahead, n, volume,
    sources, orbitals, left_ref, right_ref, waves_ref, out, *scratch,
):
    (own, mate, up, dn, src, fcol, spec, cols, back, terms, tcol, part, sums_b, sums_g, splat,
     in_sem, m_send, m_recv, up_send, up_recv, dn_send, dn_recv, s_send, s_recv,
     o_send, o_recv, f_send, f_recv, b_send, b_recv,
     t_send, t_recv, sb_send, sb_recv, sg_send, sg_recv) = scratch
    b = lax.axis_index("band")
    g = lax.axis_index("grid")
    nz = bands // 2
    z, core = b // 2, b % 2
    slab = n // grids
    depth = slab // chunks
    ycols = n // grids
    piece = ycols * depth
    yb = n // bands
    half = slab // 2
    units = half // unit
    total_units = rounds * units
    lag = (nz - 1) * ahead
    partner = z * 2 + (1 - core)

    barrier = pltpu.get_barrier_semaphore()
    for d in range(1, bands):
        pl.semaphore_signal(barrier, inc=1, device_id=(lax.rem(b + d, bands), g), device_id_type=MESH)
    for d in range(1, grids):
        pl.semaphore_signal(barrier, inc=1, device_id=(b, lax.rem(g + d, grids)), device_id_type=MESH)
    loads = [
        pltpu.make_async_copy(
            orbitals.at[0, pl.ds(h * half, half)], own.at[pl.ds(h * half, half)], in_sem.at[h]
        )
        for h in range(2)
    ]
    for load in loads:
        load.start()
    for load in loads:
        load.wait()
    pl.semaphore_wait(barrier, bands + grids - 2)

    def mate_copy(u):
        return pltpu.make_async_remote_copy(
            src_ref=own.at[pl.ds((1 - core) * half + u * unit, unit)],
            dst_ref=mate.at[pl.ds(u * unit, unit)],
            send_sem=m_send.at[u], recv_sem=m_recv.at[u],
            device_id=(partner, g), device_id_type=MESH,
        )

    def up_copy(v):
        return pltpu.make_async_remote_copy(
            src_ref=up.at[v], dst_ref=up.at[v],
            send_sem=up_send.at[v], recv_sem=up_recv.at[v],
            device_id=(lax.rem(b + 2, bands), g), device_id_type=MESH,
        )

    def dn_copy(v):
        return pltpu.make_async_remote_copy(
            src_ref=dn.at[v], dst_ref=dn.at[v],
            send_sem=dn_send.at[v], recv_sem=dn_recv.at[v],
            device_id=(lax.rem(b + bands - 2, bands), g), device_id_type=MESH,
        )

    def src_copy(v, side):
        r, u = lax.div(v, units), lax.rem(v, units)
        block = src.at[r, pl.ds(side * half + u * unit, unit)]
        return pltpu.make_async_remote_copy(
            src_ref=block, dst_ref=block,
            send_sem=s_send.at[v], recv_sem=s_recv.at[v],
            device_id=(partner, g), device_id_type=MESH,
        )

    for u in range(units):
        mate_copy(u).start()

    def step(t, _):
        @pl.when(t < units)
        def _():
            mate_copy(t).wait_recv()

        def pass_on(v, box, copy, first, last):
            @pl.when(jnp.logical_and(v >= 0, v < total_units))
            def _():
                r, u = lax.div(v, units), lax.rem(v, units)
                s = sources[r]
                here = jnp.where(
                    s == b, own[pl.ds(core * half + u * unit, unit)], mate[pl.ds(u * unit, unit)]
                )

                @pl.when(first)
                def _():
                    box[v] = here

                @pl.when(jnp.logical_not(first))
                def _():
                    copy(v).wait_recv()
                    box[v] = jnp.where(jnp.logical_or(s == b, s == partner), here, box[v])

                @pl.when(jnp.logical_not(last))
                def _():
                    copy(v).start()

        pass_on(t - z * ahead, up, up_copy, z == 0, z == nz - 1)
        pass_on(t - (nz - 1 - z) * ahead, dn, dn_copy, z == nz - 1, z == 0)
        v = t - lag

        @pl.when(v >= 0)
        def _():
            r, u = lax.div(v, units), lax.rem(v, units)
            src[r, pl.ds(core * half + u * unit, unit)] = jnp.where(
                sources[r] < 2 * z + 2, up[v], dn[v]
            )
            src_copy(v, core).start()

        return 0

    def o_copy(target, owner):
        return pltpu.make_async_remote_copy(
            src_ref=own.at[:, pl.ds(target * yb, yb)], dst_ref=fcol.at[owner],
            send_sem=o_send.at[target], recv_sem=o_recv.at[owner],
            device_id=(target, g), device_id_type=MESH,
        )

    left = left_ref[...]
    right = right_ref[...]

    def f_copy(c, r, target, owner):
        return pltpu.make_async_remote_copy(
            src_ref=spec.at[c * rounds + r, pl.ds(target * piece, piece)],
            dst_ref=cols.at[r, owner * chunks + c],
            send_sem=f_send.at[(c * rounds + r) * grids + target],
            recv_sem=f_recv.at[(c * rounds + r) * grids + owner],
            device_id=(b, target), device_id_type=MESH,
        )

    def b_copy(c, r, target, owner):
        return pltpu.make_async_remote_copy(
            src_ref=cols.at[r, target * chunks + c],
            dst_ref=back.at[c * rounds + r, pl.ds(owner * piece, piece)],
            send_sem=b_send.at[(c * rounds + r) * grids + target],
            recv_sem=b_recv.at[(c * rounds + r) * grids + owner],
            device_id=(b, target), device_id_type=MESH,
        )

    base = waves_ref[...]
    chunk_units = depth // unit

    def forward_chunk(c, r):
        for k in range(0, depth, 2):
            at = c * depth + k
            pair = src[r, pl.ds(at, 2)] * own[pl.ds(at, 2)]
            rows = along_lanes(pair.reshape(2 * n, n), right)
            planes = along_rows(left, rows[:n], rows[n:])
            spec[c * rounds + r, pl.ds(k, n, stride=depth), :] = planes[:, :n]
            spec[c * rounds + r, pl.ds(k + 1, n, stride=depth), :] = planes[:, n:]
        for d in range(1, grids):
            f_copy(c, r, lax.rem(g + d, grids), g).start()
        cols[r, g * chunks + c] = spec[c * rounds + r, pl.ds(g * piece, piece), :]

    def forward(r):
        def phase(i, _):
            start = r * units + i * chunk_units + lag
            if r == 0:
                lax.fori_loop(jnp.where(i == 0, 0, start), start + chunk_units, step, 0)
            else:
                lax.fori_loop(start, start + chunk_units, step, 0)

            def side(e, _):
                @pl.when(e == 1)
                def _():
                    for u in range(chunk_units):
                        src_copy(r * units + i * chunk_units + u, 1 - core).wait_recv()

                where = jnp.where(e == 0, core, 1 - core)
                forward_chunk(where * (chunks // 2) + i, r)
                return 0

            lax.fori_loop(0, 2, side, 0)
            return 0

        lax.fori_loop(0, chunks // 2, phase, 0)

    def lines(r):
        for c in range(chunks):
            for d in range(1, grids):
                f_copy(c, r, g, lax.rem(g + d, grids)).wait_recv()

        def line(k, _):
            held = [
                cols[r, :, pl.ds(pl.multiple_of((2 * k + e) * depth, depth), depth), :].reshape(n, n)
                for e in range(2)
            ]
            moved = along_rows(left, held[0], held[1])
            filtered = []
            for e in range(2):
                ky = g * ycols + 2 * k + e
                signed = jnp.where(ky < n // 2, ky, ky - n).astype(jnp.float32)
                wave = signed * (2.0 * math.pi / n)
                filtered.append(moved[:, e * n:(e + 1) * n] * (volume / (base + wave * wave)))
            done = along_rows(left, filtered[0], filtered[1])
            for e in range(2):
                cols[r, :, pl.ds(pl.multiple_of((2 * k + e) * depth, depth), depth), :] = (
                    done[:, e * n:(e + 1) * n].reshape(grids * chunks, depth, n)
                )
            return 0

        lax.fori_loop(0, ycols // 2, line, 0)

    def give_back(c, r):
        for d in range(1, grids):
            b_copy(c, r, lax.rem(g + d, grids), g).start()

    def inverse(c, r):
        for d in range(1, grids):
            b_copy(c, r, g, lax.rem(g + d, grids)).wait_recv()
        back[c * rounds + r, pl.ds(g * piece, piece), :] = cols[r, g * chunks + c]
        for k in range(0, depth, 2):
            planes = along_rows(
                left,
                back[c * rounds + r, pl.ds(k, n, stride=depth), :],
                back[c * rounds + r, pl.ds(k + 1, n, stride=depth), :],
            )
            rows = jnp.concatenate([planes[:, :n], planes[:, n:]], axis=0)
            potential = along_lanes(rows, right).reshape(2, n, n)
            at = c * depth + k
            here = src[r, pl.ds(at, 2)] * potential
            if r == 0:
                terms[pl.ds(at, 2)] = here
            else:
                terms[pl.ds(at, 2)] += here

    def inverse_all(r):
        def one(c, _):
            inverse(c, r)
            return 0

        lax.fori_loop(0, chunks, one, 0)

    tail = min(2, rounds)
    returned = 0
    for r in range(rounds):
        forward(r)
        if r == rounds - 1:
            for d in range(1, bands):
                o_copy(lax.rem(b + d, bands), b).start()
        if r % 2 == 1 and returned < rounds - tail:
            lines(returned)
            for c in range(chunks):
                give_back(c, returned)
            returned += 1
            ready = returned - 1
            if ready > 0:
                inverse_all(ready - 1)
    while returned < rounds - tail:
        lines(returned)
        for c in range(chunks):
            give_back(c, returned)
        returned += 1
        if returned > 1:
            inverse_all(returned - 2)
    for r in range(rounds - tail, rounds):
        lines(r)
    for c in range(chunks):
        for r in range(rounds - tail, rounds):
            give_back(c, r)
    fcol[b] = own[:, pl.ds(b * yb, yb), :]
    if rounds > tail:
        inverse_all(rounds - tail - 1)

    def t_copy(c, target, owner):
        return pltpu.make_async_remote_copy(
            src_ref=terms.at[pl.ds(c * depth, depth), pl.ds(target * yb, yb)],
            dst_ref=tcol.at[owner, pl.ds(c * depth, depth)],
            send_sem=t_send.at[c * bands + target],
            recv_sem=t_recv.at[c * bands + owner],
            device_id=(target, g), device_id_type=MESH,
        )

    def overlap(c):
        for d in range(1, bands):
            t_copy(c, b, lax.rem(b + d, bands)).wait_recv()

        def one(i, _):
            mine = fcol[i, pl.ds(c * depth, depth)]
            for k in range(bands):
                prod = mine * tcol[k, pl.ds(c * depth, depth)]
                total = jnp.sum(prod.reshape(-1, 8, n), axis=0)
                if c == 0:
                    part[i * bands + k] = total
                else:
                    part[i * bands + k] += total
            return 0

        lax.fori_loop(0, bands, one, 0)

    for c in range(chunks):
        for r in range(rounds - tail, rounds):
            inverse(c, r)
        for d in range(1, bands):
            t_copy(c, lax.rem(b + d, bands), b).start()
        tcol[b, pl.ds(c * depth, depth)] = terms[pl.ds(c * depth, depth), pl.ds(b * yb, yb), :]
        if c == 1:
            for d in range(1, bands):
                o_copy(b, lax.rem(b + d, bands)).wait_recv()
        if c > 0:
            overlap(c - 1)
    overlap(chunks - 1)

    count = bands * bands
    flat = jnp.sum(part[...], axis=1)
    if count < n:
        flat = jnp.concatenate([flat, jnp.zeros((n - count, n), jnp.float32)], axis=0)
    lanes = jnp.sum(flat.T, axis=0, keepdims=True)
    sums_b[b] = jnp.broadcast_to(lanes, (8, n))

    def sb_copy(target, owner):
        return pltpu.make_async_remote_copy(
            src_ref=sums_b.at[b], dst_ref=sums_b.at[owner],
            send_sem=sb_send.at[target], recv_sem=sb_recv.at[owner],
            device_id=(target, g), device_id_type=MESH,
        )

    def sg_copy(target, owner):
        return pltpu.make_async_remote_copy(
            src_ref=sums_g.at[g], dst_ref=sums_g.at[owner],
            send_sem=sg_send.at[target], recv_sem=sg_recv.at[owner],
            device_id=(b, target), device_id_type=MESH,
        )

    for d in range(1, bands):
        sb_copy(lax.rem(b + d, bands), b).start()
    for d in range(1, bands):
        sb_copy(b, lax.rem(b + d, bands)).wait_recv()
    sums_g[g] = jnp.sum(sums_b[...], axis=0)
    for d in range(1, grids):
        sg_copy(lax.rem(g + d, grids), g).start()
    for d in range(1, grids):
        sg_copy(g, lax.rem(g + d, grids)).wait_recv()
    total = jnp.sum(sums_g[...], axis=0)[:1] * volume
    splat[...] = jnp.broadcast_to(total, (n, n)).T

    def entry(i, k):
        first = splat[pl.ds(i * bands + k, 1), :]
        return 0.5 * (first + splat[pl.ds(k * bands + i, 1), :])

    factor = {}
    inverse_diag = {}
    for k in range(bands):
        diag = entry(k, k)
        for m in range(k):
            diag = diag - factor[k, m] * factor[k, m]
        inverse_diag[k] = 1.0 / jnp.sqrt(diag)
        for i in range(k + 1, bands):
            value = entry(i, k)
            for m in range(k):
                value = value - factor[i, m] * factor[k, m]
            factor[i, k] = value * inverse_diag[k]
    for k in range(bands):
        splat[pl.ds(k * bands + k, 1), :] = inverse_diag[k]
        for i in range(k + 1, bands):
            splat[pl.ds(i * bands + k, 1), :] = factor[i, k]

    def solve(x, _):
        solved = []
        for i in range(bands):
            value = -tcol[i, x]
            for k in range(i):
                value = value - splat[pl.ds(i * bands + k, 1), :] * solved[k]
            value = value * splat[pl.ds(i * bands + i, 1), :]
            out[i, x] = value
            solved.append(value)
        return 0

    lax.fori_loop(0, slab, solve, 0)

    for u in range(units):
        mate_copy(u).wait_send()

    def settle(v, _):
        @pl.when(z < nz - 1)
        def _():
            up_copy(v).wait_send()

        @pl.when(z > 0)
        def _():
            dn_copy(v).wait_send()

        src_copy(v, core).wait_send()
        return 0

    lax.fori_loop(0, total_units, settle, 0)
    for d in range(1, bands):
        o_copy(lax.rem(b + d, bands), b).wait_send()
    for c in range(chunks):
        for r in range(rounds):
            for d in range(1, grids):
                f_copy(c, r, lax.rem(g + d, grids), g).wait_send()
                b_copy(c, r, lax.rem(g + d, grids), g).wait_send()
        for d in range(1, bands):
            t_copy(c, lax.rem(b + d, bands), b).wait_send()
    for d in range(1, bands):
        sb_copy(lax.rem(b + d, bands), b).wait_send()
    for d in range(1, grids):
        sg_copy(lax.rem(g + d, grids), g).wait_send()


def fused(bands, grids, orbitals, sources):
    n = orbitals.shape[2]
    rounds = sources.shape[0]
    slab = n // grids
    depth = 8
    chunks = slab // depth
    yb = n // bands
    numbers = np.arange(n)
    angles = (numbers[:, None] * numbers[None, :] % n) * (2.0 * math.pi / n)
    table = jnp.asarray(np.cos(angles) + np.sin(angles), jnp.float32)
    high, low = parts_of(table)
    left = jnp.block([[high, high], [low, low]])
    right = jnp.block([[high, low], [high, low]])
    signed = np.where(numbers < n // 2, numbers, numbers - n) * (2.0 * math.pi / n)
    screen = (4.0 * math.pi / n) ** 2
    waves = jnp.asarray(signed[:, None] ** 2 + signed[None, :] ** 2 + screen, jnp.float32)
    volume = 1.0 / n**3
    f32 = jnp.float32
    dma = pltpu.SemaphoreType.DMA
    unit = 2
    units = slab // 2 // unit
    relay = rounds * units
    scratch = [
        pltpu.VMEM((slab, n, n), f32),
        pltpu.VMEM((slab // 2, n, n), f32),
        pltpu.VMEM((relay, unit, n, n), f32),
        pltpu.VMEM((relay, unit, n, n), f32),
        pltpu.VMEM((rounds, slab, n, n), f32),
        pltpu.VMEM((bands, slab, yb, n), f32),
        pltpu.VMEM((chunks * rounds, n * depth, n), f32),
        pltpu.VMEM((rounds, grids * chunks, (n // grids) * depth, n), f32),
        pltpu.VMEM((chunks * rounds, n * depth, n), f32),
        pltpu.VMEM((slab, n, n), f32),
        pltpu.VMEM((bands, slab, yb, n), f32),
        pltpu.VMEM((bands * bands, 8, n), f32),
        pltpu.VMEM((bands, 8, n), f32),
        pltpu.VMEM((grids, 8, n), f32),
        pltpu.VMEM((n, n), f32),
        dma((2,)),
        dma((units,)),
        dma((units,)),
        dma((relay,)),
        dma((relay,)),
        dma((relay,)),
        dma((relay,)),
        dma((relay,)),
        dma((relay,)),
        dma((bands,)),
        dma((bands,)),
        dma((chunks * rounds * grids,)),
        dma((chunks * rounds * grids,)),
        dma((chunks * rounds * grids,)),
        dma((chunks * rounds * grids,)),
        dma((chunks * bands,)),
        dma((chunks * bands,)),
        dma((bands,)),
        dma((bands,)),
        dma((grids,)),
        dma((grids,)),
    ]
    vmem = pl.BlockSpec(memory_space=pltpu.VMEM)
    return pl.pallas_call(
        functools.partial(whole_kernel, bands, grids, rounds, chunks, unit, 2, n, volume),
        out_shape=jax.ShapeDtypeStruct((bands, slab, yb, n), f32),
        in_specs=[
            pl.BlockSpec(memory_space=pltpu.SMEM),
            pl.BlockSpec(memory_space=pl.ANY),
            vmem, vmem, vmem,
        ],
        out_specs=vmem,
        scratch_shapes=scratch,
        compiler_params=pltpu.CompilerParams(
            collective_id=0, has_side_effects=True, vmem_limit_bytes=60 * 1024 * 1024
        ),
        name="exchange",
    )(sources, orbitals, left, right, waves)


def per_device(orbitals, sources):
    held, slab, full_y, full_z = orbitals.shape
    bands = lax.axis_size("band")
    grids = lax.axis_size("grid")
    n = full_y
    fits = (
        held == 1 and n == full_z == slab * grids and n % 128 == 0 and slab % 16 == 0
        and bands % 2 == 0 and bands * bands <= n and n % (8 * bands) == 0
        and 4 * n * n * slab * (5 * sources.shape[0] + 6) <= 54 * 2**20
    )
    if fits:
        return fused(bands, grids, orbitals, sources)
    return general(orbitals, sources)


def solution(mesh):
    placed = (P("band", "grid", None, None), P())
    return jax.shard_map(
        per_device,
        mesh=mesh,
        in_specs=placed,
        out_specs=P(None, "grid", "band", None),
        check_vma=False,
    )
```

profile of v0, /device:TPU:0, one launch (start us, length us, event | category | flops | bytes accessed | tf_op | source)
XLA Modules:
  0.0 246.0 jit_solution(13523174290146528296)
XLA Ops:
  0.0 243.0 %exchange.1 = f32[8,32,16,128]{3,2,1,0:T(8,128)} custom-call(s32[4]{0:T(128)} %sources.1, f32[1,32,128,128]{3,2,1,0:T(8,128)} %orbitals.1, bf16[256,256]{1,0:T(8,128)(2,1)} %constant.13.left_ref, bf16[256,256]{1,0:T(8,128)(2,1)} %constant.15.right_ref, f32[128,128]{1,0:T(8,128)} %constant.5.clone.waves_ref), custom_call_target="tpu_custom_call" | custom-call | tf_op jit(solution)/shard_map/exchange/pallas_call | solution.py:588
  243.0 3.0 %copy.6 = f32[8,32,16,128]{3,2,1,0:T(8,128)} copy(f32[8,32,16,128]{3,2,1,0:T(8,128)} %exchange.1) | data formatting | bytes 4194304
where the time goes:
time: 246 us
  Pallas kernels  243 us (99%)
  local copies, waits for them, and re-layouts  3.05 us (1%)
    pallas_call x1, Pallas kernels, fused(): pl.pallas_call(functools.partial(whole_kernel, bands, grids, rounds, chun...  243 us

commit v1 on v0

--- a/solution.py
+++ b/solution.py
@@ -120,7 +120,7 @@
 
 
 def whole_kernel(
-    bands, grids, rounds, chunks, unit, ahead, n, volume,
+    bands, grids, rounds, chunks, ahead, slack, n, volume,
     sources, orbitals, left_ref, right_ref, waves_ref, out, *scratch,
 ):
     (own, mate, up, dn, src, fcol, spec, cols, back, terms, tcol, part, sums_b, sums_g, splat,
@@ -137,7 +137,8 @@
     piece = ycols * depth
     yb = n // bands
     half = slab // 2
-    units = half // unit
+    units = half
+    per = depth // 2
     total_units = rounds * units
     lag = (nz - 1) * ahead
     partner = z * 2 + (1 - core)
@@ -161,8 +162,8 @@
 
     def mate_copy(u):
         return pltpu.make_async_remote_copy(
-            src_ref=own.at[pl.ds((1 - core) * half + u * unit, unit)],
-            dst_ref=mate.at[pl.ds(u * unit, unit)],
+            src_ref=own.at[2 * u + 1 - core],
+            dst_ref=mate.at[u],
             send_sem=m_send.at[u], recv_sem=m_recv.at[u],
             device_id=(partner, g), device_id_type=MESH,
         )
@@ -183,15 +184,18 @@
 
     def src_copy(v, side):
         r, u = lax.div(v, units), lax.rem(v, units)
-        block = src.at[r, pl.ds(side * half + u * unit, unit)]
+        block = src.at[r, 2 * u + side]
         return pltpu.make_async_remote_copy(
             src_ref=block, dst_ref=block,
             send_sem=s_send.at[v], recv_sem=s_recv.at[v],
             device_id=(partner, g), device_id_type=MESH,
         )
 
-    for u in range(units):
+    def mate_start(u, _):
         mate_copy(u).start()
+        return 0
+
+    lax.fori_loop(0, units, mate_start, 0)
 
     def step(t, _):
         @pl.when(t < units)
@@ -204,7 +208,7 @@
                 r, u = lax.div(v, units), lax.rem(v, units)
                 s = sources[r]
                 here = jnp.where(
-                    s == b, own[pl.ds(core * half + u * unit, unit)], mate[pl.ds(u * unit, unit)]
+                    s == b, own[2 * u + core], mate[u]
                 )
 
                 @pl.when(first)
@@ -224,10 +228,10 @@
         pass_on(t - (nz - 1 - z) * ahead, dn, dn_copy, z == nz - 1, z == 0)
         v = t - lag
 
-        @pl.when(v >= 0)
+        @pl.when(jnp.logical_and(v >= 0, v < total_units))
         def _():
             r, u = lax.div(v, units), lax.rem(v, units)
-            src[r, pl.ds(core * half + u * unit, unit)] = jnp.where(
+            src[r, 2 * u + core] = jnp.where(
                 sources[r] < 2 * z + 2, up[v], dn[v]
             )
             src_copy(v, core).start()
@@ -263,7 +267,6 @@
         )
 
     base = waves_ref[...]
-    chunk_units = depth // unit
 
     def forward_chunk(c, r):
         for k in range(0, depth, 2):
@@ -278,27 +281,17 @@
         cols[r, g * chunks + c] = spec[c * rounds + r, pl.ds(g * piece, piece), :]
 
     def forward(r):
-        def phase(i, _):
-            start = r * units + i * chunk_units + lag
-            if r == 0:
-                lax.fori_loop(jnp.where(i == 0, 0, start), start + chunk_units, step, 0)
-            else:
-                lax.fori_loop(start, start + chunk_units, step, 0)
-
-            def side(e, _):
-                @pl.when(e == 1)
-                def _():
-                    for u in range(chunk_units):
-                        src_copy(r * units + i * chunk_units + u, 1 - core).wait_recv()
-
-                where = jnp.where(e == 0, core, 1 - core)
-                forward_chunk(where * (chunks // 2) + i, r)
-                return 0
-
-            lax.fori_loop(0, 2, side, 0)
+        def chunk(c, _):
+            first = r * units + c * per
+            done = first + lag + slack
+            begin = jnp.where(c == 0, 0, done) if r == 0 else done
+            lax.fori_loop(begin, done + per, step, 0)
+            for e in range(per):
+                src_copy(first + e, 1 - core).wait_recv()
+            forward_chunk(c, r)
             return 0
 
-        lax.fori_loop(0, chunks // 2, phase, 0)
+        lax.fori_loop(0, chunks, chunk, 0)
 
     def lines(r):
         for c in range(chunks):
@@ -493,8 +486,11 @@
 
     lax.fori_loop(0, slab, solve, 0)
 
-    for u in range(units):
+    def mate_settle(u, _):
         mate_copy(u).wait_send()
+        return 0
+
+    lax.fori_loop(0, units, mate_settle, 0)
 
     def settle(v, _):
         @pl.when(z < nz - 1)
@@ -543,14 +539,13 @@
     volume = 1.0 / n**3
     f32 = jnp.float32
     dma = pltpu.SemaphoreType.DMA
-    unit = 2
-    units = slab // 2 // unit
+    units = slab // 2
     relay = rounds * units
     scratch = [
         pltpu.VMEM((slab, n, n), f32),
         pltpu.VMEM((slab // 2, n, n), f32),
-        pltpu.VMEM((relay, unit, n, n), f32),
-        pltpu.VMEM((relay, unit, n, n), f32),
+        pltpu.VMEM((relay, n, n), f32),
+        pltpu.VMEM((relay, n, n), f32),
         pltpu.VMEM((rounds, slab, n, n), f32),
         pltpu.VMEM((bands, slab, yb, n), f32),
         pltpu.VMEM((chunks * rounds, n * depth, n), f32),
@@ -586,7 +581,7 @@
     ]
     vmem = pl.BlockSpec(memory_space=pltpu.VMEM)
     return pl.pallas_call(
-        functools.partial(whole_kernel, bands, grids, rounds, chunks, unit, 2, n, volume),
+        functools.partial(whole_kernel, bands, grids, rounds, chunks, 3, 1, n, volume),
         out_shape=jax.ShapeDtypeStruct((bands, slab, yb, n), f32),
         in_specs=[
             pl.BlockSpec(memory_space=pltpu.SMEM),

time: 246 us -> 244 us (level)
  Pallas kernels: 243 us -> 240 us
    pallas_call x1, Pallas kernels: 243 us -> 240 us  [fused(): pl.pallas_call(functools.partial(whole_kernel, bands, grids, rounds, chun...]
where the time goes in v1:
time: 244 us
  Pallas kernels  240 us (98%)
  local copies, waits for them, and re-layouts  3.05 us (1%)
    pallas_call x1, Pallas kernels, fused(): pl.pallas_call(functools.partial(whole_kernel, bands, grids, rounds, chun...  240 us

profile of v1, /device:TPU:0, one launch (start us, length us, event | category | flops | bytes accessed | tf_op | source)
XLA Modules:
  0.0 243.5 jit_solution(17849733969339718964)
XLA Ops:
  0.0 240.5 %exchange.1 = f32[8,32,16,128]{3,2,1,0:T(8,128)} custom-call(s32[4]{0:T(128)} %sources.1, f32[1,32,128,128]{3,2,1,0:T(8,128)} %orbitals.1, bf16[256,256]{1,0:T(8,128)(2,1)} %constant.13.left_ref, bf16[256,256]{1,0:T(8,128)(2,1)} %constant.15.right_ref, f32[128,128]{1,0:T(8,128)} %constant.5.clone.waves_ref), custom_call_target="tpu_custom_call" | custom-call | tf_op jit(solution)/shard_map/exchange/pallas_call | solution.py:583
  240.5 3.0 %copy.6 = f32[8,32,16,128]{3,2,1,0:T(8,128)} copy(f32[8,32,16,128]{3,2,1,0:T(8,128)} %exchange.1) | data formatting | bytes 4194304

commit v2 on v1

v2 whole, which is shorter than its diff:
```python
import functools
import math

import jax
import jax.numpy as jnp
import numpy as np
from jax import lax
from jax.experimental import pallas as pl
from jax.experimental.pallas import tpu as pltpu
from jax.sharding import PartitionSpec as P

highest = lax.Precision.HIGHEST
MESH = pl.DeviceIdType.MESH


def spread_2(block, axis, owner):
    block = jnp.where(lax.axis_index(axis) == owner, block, jnp.zeros_like(block))
    return lax.psum(block, axis)


def cas_table(length):
    index_values = jnp.arange(length, dtype=jnp.int32)
    products = index_values[:, None] * index_values[None, :] % length
    angles = products.astype(jnp.float32) * (2.0 * math.pi / length)
    return jnp.cos(angles) + jnp.sin(angles)


def squared_waves(start, count, length):
    index_values = start + jnp.arange(count, dtype=jnp.int32)
    signed = jnp.where(index_values < length // 2, index_values, index_values - length)
    waves = signed.astype(jnp.float32) * (2.0 * math.pi / length)
    return waves * waves


def general(orbitals, sources):
    band_count, slab_x, full_y, full_z = orbitals.shape
    grid_count = lax.axis_size("grid")
    full_x = slab_x * grid_count
    total_bands = band_count * lax.axis_size("band")
    round_count = sources.shape[0]
    table_x = cas_table(full_x)
    table_y = cas_table(full_y)
    table_z = cas_table(full_z)
    column_y = full_y // grid_count
    start_y = lax.axis_index("grid") * column_y
    waves = (
        squared_waves(0, full_x, full_x)[:, None, None]
        + squared_waves(start_y, column_y, full_y)[None, :, None]
        + squared_waves(0, full_z, full_z)[None, None, :]
    )
    screen = (4.0 * math.pi / full_x) ** 2
    volume = 1.0 / (full_x * full_y * full_z)
    kernel = volume / (waves + screen)

    def plane_transform(field):
        spread = jnp.einsum("bxyz,zk->bxyk", field, table_z, precision=highest)
        return jnp.einsum("bxyk,yj->bxjk", spread, table_y, precision=highest)

    def own_slab(number):
        owner = number // band_count
        local = number % band_count
        return (owner, lax.dynamic_index_in_dim(orbitals, local, 0, keepdims=False))

    def fetch(number):
        owner, slab = own_slab(number)
        return spread_2(slab, "band", owner)

    arrived = [fetch(sources[turn]) for turn in range(round_count)]
    terms = jnp.zeros(orbitals.shape, jnp.float32)
    for turn in range(round_count):
        source = arrived[turn][None]
        spectra = plane_transform(orbitals * source)
        potential_columns = lax.all_to_all(spectra, "grid", split_axis=2, concat_axis=1, tiled=True)
        line_spread = jnp.einsum("bxyz,xa->bayz", potential_columns, table_x, precision=highest)
        line_spread = line_spread * kernel[None]
        filtered = jnp.einsum("bayz,ax->bxyz", line_spread, table_x, precision=highest)
        terms = terms + source * plane_transform(
            lax.all_to_all(filtered, "grid", split_axis=1, concat_axis=2, tiled=True)
        )
    orbital_cols, term_cols = (
        lax.all_to_all(orbitals, "band", split_axis=2, concat_axis=0, tiled=True),
        lax.all_to_all(terms, "band", split_axis=2, concat_axis=0, tiled=True),
    )
    flat_orbitals = orbital_cols.reshape(total_bands, -1)
    flat_terms = term_cols.reshape(total_bands, -1)
    partial_intersection = (
        jnp.dot(flat_orbitals, flat_terms.T, precision=highest, preferred_element_type=jnp.float32)
        * volume
    )
    intersection = lax.psum(partial_intersection, ("band", "grid"))
    factor = jnp.linalg.cholesky(intersection)
    solved = lax.linalg.triangular_solve(factor, flat_terms, left_side=True, lower=True)
    return (-solved).reshape(term_cols.shape)


def parts_of(value):
    high = value.astype(jnp.bfloat16)
    low = (value - high.astype(jnp.float32)).astype(jnp.bfloat16)
    return high, low


def along_rows(left, first, second):
    n = first.shape[0]
    h0, l0 = parts_of(first)
    h1, l1 = parts_of(second)
    right = jnp.concatenate(
        [jnp.concatenate([h0, h1], axis=1), jnp.concatenate([l0, l1], axis=1)], axis=0
    )
    both = jnp.dot(left, right, preferred_element_type=jnp.float32)
    return both[:n] + both[n:]


def along_lanes(rows, right):
    n = rows.shape[1]
    high, low = parts_of(rows)
    both = jnp.dot(
        jnp.concatenate([high, low], axis=1), right, preferred_element_type=jnp.float32
    )
    return both[:, :n] + both[:, n:]


def pick(i, values):
    out = values[-1]
    for m in reversed(range(len(values) - 1)):
        out = jnp.where(i == m, values[m], out)
    return out


def whole_kernel(
    bands, grids, rounds, ahead, depth, n, volume,
    sources, orbitals, left_ref, right_ref, waves_ref, out, *scratch,
):
    (own, orb, up, dn, src, fcol, spec, cols, back, terms, pin, tcol, part, sums_b, sums_g, splat,
     in_sem, m_send, m_recv, ox_send, ox_recv, oy_send, oy_recv, or_send, or_recv,
     up_send, up_recv, dn_send, dn_recv, y_send, y_recv, o_send, o_recv, f_send, f_recv,
     b_send, b_recv, p_send, p_recv, t_send, t_recv,
     sb_send, sb_recv, sg_send, sg_recv) = scratch
    b = lax.axis_index("band")
    g = lax.axis_index("grid")
    nz = bands // 2
    z, core = b // 2, b % 2
    slab = n // grids
    half = slab // 2
    yb = n // bands
    pieces = half // depth
    slots = grids * pieces
    quarter = half // 4
    mine = n // 2 * depth
    phases = rounds // 2
    total_units = phases * 2 * half
    lag = (nz - 1) * ahead
    partner = z * 2 + (1 - core)
    gx = g + 1 - 2 * (g % 2)
    gy = lax.rem(g + 2, grids)
    gd = gx + 2 - 4 * (gx // 2)
    column, row = g % 2, g // 2

    barrier = pltpu.get_barrier_semaphore()
    for d in range(1, bands):
        pl.semaphore_signal(barrier, inc=1, device_id=(lax.rem(b + d, bands), g), device_id_type=MESH)
    for d in range(bands):
        pl.semaphore_signal(barrier, inc=1, device_id=(lax.rem(b + d, bands), gy), device_id_type=MESH)
    pl.semaphore_signal(barrier, inc=1, device_id=(b, gx), device_id_type=MESH)
    pl.semaphore_signal(barrier, inc=1, device_id=(b, gd), device_id_type=MESH)
    loads = [
        pltpu.make_async_copy(
            orbitals.at[0, pl.ds((1 - core) * half, half)], own.at[pl.ds((1 - core) * half, half)],
            in_sem.at[0],
        ),
        pltpu.make_async_copy(
            orbitals.at[0, pl.ds(core * half, half)], orb.at[core, g], in_sem.at[1]
        ),
        pltpu.make_async_copy(
            orbitals.at[0, pl.ds(core * half, half)], own.at[pl.ds(core * half, half)], in_sem.at[2]
        ),
    ]
    for load in loads:
        load.start()
    for load in loads:
        load.wait()
    pl.semaphore_wait(barrier, 2 * bands + 1)

    def mate_copy(u, parity):
        return pltpu.make_async_remote_copy(
            src_ref=own.at[pl.ds((1 - core) * half + u * quarter, quarter)],
            dst_ref=orb.at[parity, g, pl.ds(u * quarter, quarter)],
            send_sem=m_send.at[u], recv_sem=m_recv.at[u],
            device_id=(partner, g), device_id_type=MESH,
        )

    def ox_copy(u, which, owner):
        block = orb.at[which, owner, pl.ds(u * quarter, quarter)]
        return pltpu.make_async_remote_copy(
            src_ref=block, dst_ref=block,
            send_sem=ox_send.at[2 * u + which], recv_sem=ox_recv.at[2 * u + which],
            device_id=(b, gx), device_id_type=MESH,
        )

    def oy_copy(u, which, owner):
        block = orb.at[which, owner, pl.ds(u * quarter, quarter)]
        return pltpu.make_async_remote_copy(
            src_ref=block, dst_ref=block,
            send_sem=oy_send.at[u], recv_sem=oy_recv.at[u],
            device_id=(b, gy), device_id_type=MESH,
        )

    def or_copy(u, owner):
        block = orb.at[row, owner, pl.ds(u * quarter, quarter)]
        return pltpu.make_async_remote_copy(
            src_ref=block, dst_ref=block,
            send_sem=or_send.at[u], recv_sem=or_recv.at[u],
            device_id=(b, gx), device_id_type=MESH,
        )

    def up_copy(v):
        return pltpu.make_async_remote_copy(
            src_ref=up.at[v], dst_ref=up.at[v],
            send_sem=up_send.at[v], recv_sem=up_recv.at[v],
            device_id=(lax.rem(b + 2, bands), g), device_id_type=MESH,
        )

    def dn_copy(v):
        return pltpu.make_async_remote_copy(
            src_ref=dn.at[v], dst_ref=dn.at[v],
            send_sem=dn_send.at[v], recv_sem=dn_recv.at[v],
            device_id=(lax.rem(b + bands - 2, bands), g), device_id_type=MESH,
        )

    def place(v):
        q = lax.div(v, 2 * half)
        side = lax.rem(lax.div(v, half), 2)
        return q, side, lax.rem(v, half)

    def y_copy(v, near, far):
        q, side, u = place(v)
        block = src.at[q, jnp.where(side == 0, near, far), u]
        return pltpu.make_async_remote_copy(
            src_ref=block, dst_ref=block,
            send_sem=y_send.at[v], recv_sem=y_recv.at[v],
            device_id=(b, gy), device_id_type=MESH,
        )

    for u in range(4):
        mate_copy(u, core).start()
    for u in range(4):
        mate_copy(u, 1 - core).wait_recv()
        oy_copy(u, 1 - row, g).start()
        for which in range(2):
            ox_copy(u, which, g).start()

    def step(t, _):
        @pl.when(jnp.logical_and(t >= half, jnp.logical_and(t < 2 * half, lax.rem(t, quarter) == 0)))
        def _():
            u = lax.div(t - half, quarter)
            for which in range(2):
                ox_copy(u, which, gx).wait_recv()

        for u in range(4):
            @pl.when(t == quarter * (u + 1) + 3)
            def _():
                oy_copy(u, row, gy).wait_recv()
                or_copy(u, gy).start()

        def pass_on(v, box, copy, first, last):
            @pl.when(jnp.logical_and(v >= 0, v < total_units))
            def _():
                q, side, u = place(v)
                s = sources[phases * column + q]
                at = jnp.where(side == 0, g, gx)
                here = jnp.where(lax.rem(s, 2) == 0, orb[0, at, u], orb[1, at, u])

                @pl.when(first)
                def _():
                    box[v] = here

                @pl.when(jnp.logical_not(first))
                def _():
                    copy(v).wait_recv()
                    box[v] = jnp.where(lax.div(s, 2) == z, here, box[v])

                @pl.when(jnp.logical_not(last))
                def _():
                    copy(v).start()

        pass_on(t - z * ahead, up, up_copy, z == 0, z == nz - 1)
        pass_on(t - (nz - 1 - z) * ahead, dn, dn_copy, z == nz - 1, z == 0)
        v = t - lag

        @pl.when(jnp.logical_and(v >= 0, v < total_units))
        def _():
            q, side, u = place(v)
            s = sources[phases * column + q]
            src[q, jnp.where(side == 0, g, gx), u] = jnp.where(s < 2 * z + 2, up[v], dn[v])
            y_copy(v, g, gx).start()

        return 0

    left = left_ref[...]
    right = right_ref[...]
    base = waves_ref[...]

    def f_copy(q, at, piece, side):
        slot = at * pieces + piece
        return pltpu.make_async_remote_copy(
            src_ref=spec.at[slot, pl.ds((1 - core) * mine, mine)],
            dst_ref=cols.at[q, (at * 2 + side) * pieces + piece],
            send_sem=f_send.at[q * slots + slot], recv_sem=f_recv.at[q * slots + slot],
            device_id=(partner, g), device_id_type=MESH,
        )

    def b_copy(q, at, piece, side):
        slot = at * pieces + piece
        return pltpu.make_async_remote_copy(
            src_ref=cols.at[q, (at * 2 + 1 - side) * pieces + piece],
            dst_ref=back.at[q, slot, pl.ds(side * mine, mine)],
            send_sem=b_send.at[q * slots + slot], recv_sem=b_recv.at[q * slots + slot],
            device_id=(partner, g), device_id_type=MESH,
        )

    order = [(g, 0), (g, 1), (gy, 0), (gx, 0), (gy, 1), (gx, 1), (gd, 0), (gd, 1)]

    def forward(q, i):
        at = pick(i, [a for a, _ in order])
        piece = pick(i, [p for _, p in order])
        far = at == gd

        @pl.when(jnp.logical_or(far, at == gy))
        def _():
            start = q * 2 * half + jnp.where(far, half, 0) + piece * depth

            def arrive(e, _):
                y_copy(start + e, gy, gd).wait_recv()
                return 0

            lax.fori_loop(0, depth, arrive, 0)

        if q == 0:
            @pl.when(far)
            def _():
                for e in range(2):
                    or_copy(2 * piece + e, gd).wait_recv()

        slot = at * pieces + piece
        if q > 0:
            f_copy(q - 1, at, piece, core).wait_send()
        for k in range(0, depth, 2):
            here = pl.ds(piece * depth + k, 2)
            pair = src[q, at, here] * orb[row, at, here]
            rows = along_lanes(pair.reshape(2 * n, n), right)
            planes = along_rows(left, rows[:n], rows[n:])
            spec[slot, pl.ds(k, n, stride=depth), :] = planes[:, :n]
            spec[slot, pl.ds(k + 1, n, stride=depth), :] = planes[:, n:]
        f_copy(q, at, piece, core).start()
        cols[q, (at * 2 + core) * pieces + piece] = spec[slot, pl.ds(core * mine, mine), :]

    def every(q, copy_of):
        for at in range(grids):
            for piece in range(pieces):
                copy_of(q, at, piece)

    lines_count = n // 4

    def lines(q, first, count):
        def line(k, _):
            held = [
                cols[q, :, pl.ds(pl.multiple_of((2 * k + e) * depth, depth), depth), :].reshape(n, n)
                for e in range(2)
            ]
            moved = along_rows(left, held[0], held[1])
            filtered = []
            for e in range(2):
                ky = core * (n // 2) + 2 * k + e
                signed = jnp.where(ky < n // 2, ky, ky - n).astype(jnp.float32)
                wave = signed * (2.0 * math.pi / n)
                filtered.append(moved[:, e * n:(e + 1) * n] * (volume / (base + wave * wave)))
            done = along_rows(left, filtered[0], filtered[1])
            for e in range(2):
                cols[q, :, pl.ds(pl.multiple_of((2 * k + e) * depth, depth), depth), :] = (
                    done[:, e * n:(e + 1) * n].reshape(n // depth, depth, n)
                )
            return 0

        lax.fori_loop(first, first + count, line, 0)

    def inverse(q, at, piece):
        slot = at * pieces + piece
        b_copy(q, at, piece, 1 - core).wait_recv()
        back[q, slot, pl.ds(core * mine, mine), :] = cols[q, (at * 2 + core) * pieces + piece]
        for k in range(0, depth, 2):
            planes = along_rows(
                left,
                back[q, slot, pl.ds(k, n, stride=depth), :],
                back[q, slot, pl.ds(k + 1, n, stride=depth), :],
            )
            rows = jnp.concatenate([planes[:, :n], planes[:, n:]], axis=0)
            potential = along_lanes(rows, right).reshape(2, n, n)
            here = pl.ds(piece * depth + k, 2)
            value = src[q, at, here] * potential
            if q == 0:
                terms[at, here] = value
            else:
                terms[at, here] += value

    def o_copy(target, owner):
        return pltpu.make_async_remote_copy(
            src_ref=own.at[:, pl.ds(target * yb, yb)], dst_ref=fcol.at[owner],
            send_sem=o_send.at[target], recv_sem=o_recv.at[owner],
            device_id=(target, g), device_id_type=MESH,
        )

    def p_copy(at, side, m):
        return pltpu.make_async_remote_copy(
            src_ref=terms.at[at, pl.ds(m * quarter, quarter)],
            dst_ref=pin.at[side, pl.ds(m * quarter, quarter)],
            send_sem=p_send.at[side * 4 + m], recv_sem=p_recv.at[side * 4 + m],
            device_id=(b, gx), device_id_type=MESH,
        )

    def bounds(q, remote):
        local = [q * 2 * half + lag + side * half + (p + 1) * depth for side in range(2) for p in range(2)]
        far = [at + remote for at in local]
        return [local[0], local[1], far[0], local[2], far[1], local[3], far[2], far[3]]

    first_bounds = bounds(0, 10)
    second_bounds = bounds(1, 10)

    def advance(start, stop):
        lax.fori_loop(start, stop, step, 0)

    def first_forward(i, at):
        stop = pick(i, first_bounds)
        advance(at, stop)
        forward(0, i)
        return stop

    at = lax.fori_loop(0, slots, first_forward, 0)
    advance(first_bounds[-1], first_bounds[-1] + 2)
    every(0, lambda q, at, piece: f_copy(q, at, piece, 1 - core).wait_recv())
    settle = first_bounds[-1] + 2

    def first_lines(i, _):
        lines(0, i * (lines_count // slots), lines_count // slots)
        advance(settle + i, settle + i + 1)
        return 0

    lax.fori_loop(0, slots, first_lines, 0)
    every(0, lambda q, at, piece: b_copy(q, at, piece, core).start())
    reached = settle + slots

    def second_forward(i, at):
        stop = jnp.maximum(pick(i, second_bounds), at)
        advance(at, stop)
        inverse(0, lax.div(i, pieces), lax.rem(i, pieces))
        forward(1, i)

        @pl.when(i == 5)
        def _():
            for d in range(1, bands):
                o_copy(lax.rem(b + d, bands), b).start()

        return stop

    lax.fori_loop(0, slots, second_forward, reached)
    every(1, lambda q, at, piece: f_copy(q, at, piece, 1 - core).wait_recv())
    lines(1, 0, lines_count)
    every(1, lambda q, at, piece: b_copy(q, at, piece, core).start())

    fcol[b] = own[:, pl.ds(b * yb, yb), :]
    part[...] = jnp.zeros_like(part)

    def second_inverse(i, _):
        at = pick(lax.div(i, pieces), [gd, gx, gy, g])
        piece = lax.rem(i, pieces)
        inverse(1, at, piece)

        @pl.when(i < 2 * pieces)
        def _():
            for e in range(2):
                p_copy(at, lax.div(i, pieces), 2 * piece + e).start()

        return 0

    lax.fori_loop(0, slots, second_inverse, 0)

    orbital = 2 * z + row

    def t_copy(m, at, target):
        rows = pl.ds(m * quarter, quarter)
        return pltpu.make_async_remote_copy(
            src_ref=terms.at[at, rows, pl.ds(target * yb, yb)],
            dst_ref=tcol.at[orbital, pl.ds(core * half + m * quarter, quarter)],
            send_sem=t_send.at[(jnp.where(at == g, 1, 0) * 4 + m) * bands + target],
            recv_sem=t_recv.at[(orbital * 2 + core) * 4 + m],
            device_id=(target, at), device_id_type=MESH,
        )

    def t_arrival(m, which, side):
        block = tcol.at[which, pl.ds(side * half + m * quarter, quarter)]
        return pltpu.make_async_remote_copy(
            src_ref=block, dst_ref=block,
            send_sem=t_send.at[0], recv_sem=t_recv.at[(which * 2 + side) * 4 + m],
            device_id=(partner, g), device_id_type=MESH,
        )

    def finish(i, _):
        @pl.when(i < 8)
        def _():
            own_side = lax.div(i, 4)
            m = lax.rem(i, 4)
            at = jnp.where(own_side == 0, gy, g)
            rows = pl.ds(m * quarter, quarter)
            p_copy(at, own_side, m).wait_recv()
            terms[at, rows] += pin[own_side, rows]

            @pl.when(own_side == 0)
            def _():
                for target in range(bands):
                    t_copy(m, gy, target).start()

            @pl.when(own_side == 1)
            def _():
                for d in range(1, bands):
                    t_copy(m, g, lax.rem(b + d, bands)).start()
                tcol[orbital, pl.ds(core * half + m * quarter, quarter)] = terms[
                    g, rows, pl.ds(b * yb, yb), :
                ]

        @pl.when(i == 2)
        def _():
            for d in range(1, bands):
                o_copy(b, lax.rem(b + d, bands)).wait_recv()

        @pl.when(i >= 2)
        def _():
            own_side = lax.div(i - 2, 4)
            m = lax.rem(i - 2, 4)
            parity = jnp.where(own_side == 0, 1 - row, row)
            for k in range(nz):
                for side in range(2):
                    local = jnp.logical_and(
                        jnp.logical_and(own_side == 1, z == k), core == side
                    )

                    @pl.when(jnp.logical_not(local))
                    def _():
                        t_arrival(m, 2 * k + parity, side).wait_recv()

            def one(a, _):
                held = [fcol[a, pl.ds(side * half + m * quarter, quarter)] for side in range(2)]
                for k in range(nz):
                    which = 2 * k + parity
                    total = jnp.zeros((8, n), jnp.float32)
                    for side in range(2):
                        prod = held[side] * tcol[which, pl.ds(side * half + m * quarter, quarter)]
                        total = total + jnp.sum(prod.reshape(-1, 8, n), axis=0)
                    part[a * bands + which] += total
                return 0

            lax.fori_loop(0, bands, one, 0)

        return 0

    lax.fori_loop(0, 10, finish, 0)

    count = bands * bands
    flat = jnp.sum(part[...], axis=1)
    if count < n:
        flat = jnp.concatenate([flat, jnp.zeros((n - count, n), jnp.float32)], axis=0)
    lanes = jnp.sum(flat.T, axis=0, keepdims=True)
    sums_b[b] = jnp.broadcast_to(lanes, (8, n))

    def sb_copy(target, owner):
        return pltpu.make_async_remote_copy(
            src_ref=sums_b.at[b], dst_ref=sums_b.at[owner],
            send_sem=sb_send.at[target], recv_sem=sb_recv.at[owner],
            device_id=(target, g), device_id_type=MESH,
        )

    def sg_copy(target, owner):
        return pltpu.make_async_remote_copy(
            src_ref=sums_g.at[g], dst_ref=sums_g.at[owner],
            send_sem=sg_send.at[target], recv_sem=sg_recv.at[owner],
            device_id=(b, target), device_id_type=MESH,
        )

    for d in range(1, bands):
        sb_copy(lax.rem(b + d, bands), b).start()
    for d in range(1, bands):
        sb_copy(b, lax.rem(b + d, bands)).wait_recv()
    sums_g[g] = jnp.sum(sums_b[...], axis=0)
    for d in range(1, grids):
        sg_copy(lax.rem(g + d, grids), g).start()
    for d in range(1, grids):
        sg_copy(g, lax.rem(g + d, grids)).wait_recv()
    total = jnp.sum(sums_g[...], axis=0)[:1] * volume
    splat[...] = jnp.broadcast_to(total, (n, n)).T

    def entry(i, k):
        first = splat[pl.ds(i * bands + k, 1), :]
        return 0.5 * (first + splat[pl.ds(k * bands + i, 1), :])

    factor = {}
    inverse_diag = {}
    for k in range(bands):
        diag = entry(k, k)
        for m in range(k):
            diag = diag - factor[k, m] * factor[k, m]
        inverse_diag[k] = 1.0 / jnp.sqrt(diag)
        for i in range(k + 1, bands):
            value = entry(i, k)
            for m in range(k):
                value = value - factor[i, m] * factor[k, m]
            factor[i, k] = value * inverse_diag[k]
    for k in range(bands):
        splat[pl.ds(k * bands + k, 1), :] = inverse_diag[k]
        for i in range(k + 1, bands):
            splat[pl.ds(i * bands + k, 1), :] = factor[i, k]

    def solve(p, _):
        x = pl.ds(4 * p, 4)
        solved = []
        for i in range(bands):
            value = -tcol[i, x]
            for k in range(i):
                value = value - splat[pl.ds(i * bands + k, 1), :] * solved[k]
            value = value * splat[pl.ds(i * bands + i, 1), :]
            out[i, x] = value
            solved.append(value)
        return 0

    lax.fori_loop(0, slab // 4, solve, 0)

    for u in range(4):
        mate_copy(u, core).wait_send()
        oy_copy(u, 1 - row, g).wait_send()
        or_copy(u, gy).wait_send()
        for which in range(2):
            ox_copy(u, which, g).wait_send()

    def settle_units(v, _):
        @pl.when(z < nz - 1)
        def _():
            up_copy(v).wait_send()

        @pl.when(z > 0)
        def _():
            dn_copy(v).wait_send()

        y_copy(v, g, gx).wait_send()
        return 0

    lax.fori_loop(0, total_units, settle_units, 0)
    every(phases - 1, lambda q, at, piece: f_copy(q, at, piece, core).wait_send())
    for q in range(phases):
        every(q, lambda q, at, piece: b_copy(q, at, piece, core).wait_send())
    for m in range(4):
        p_copy(gd, 0, m).wait_send()
        p_copy(gx, 1, m).wait_send()
        for target in range(bands):
            t_copy(m, gy, target).wait_send()
        for d in range(1, bands):
            t_copy(m, g, lax.rem(b + d, bands)).wait_send()
    for d in range(1, bands):
        o_copy(lax.rem(b + d, bands), b).wait_send()
        sb_copy(lax.rem(b + d, bands), b).wait_send()
    for d in range(1, grids):
        sg_copy(lax.rem(g + d, grids), g).wait_send()


def fused(bands, grids, orbitals, sources):
    n = orbitals.shape[2]
    rounds = sources.shape[0]
    slab = n // grids
    half = slab // 2
    depth = 8
    pieces = half // depth
    slots = grids * pieces
    phases = rounds // 2
    yb = n // bands
    numbers = np.arange(n)
    angles = (numbers[:, None] * numbers[None, :] % n) * (2.0 * math.pi / n)
    table = jnp.asarray(np.cos(angles) + np.sin(angles), jnp.float32)
    high, low = parts_of(table)
    left = jnp.block([[high, high], [low, low]])
    right = jnp.block([[high, low], [high, low]])
    signed = np.where(numbers < n // 2, numbers, numbers - n) * (2.0 * math.pi / n)
    screen = (4.0 * math.pi / n) ** 2
    waves = jnp.asarray(signed[:, None] ** 2 + signed[None, :] ** 2 + screen, jnp.float32)
    volume = 1.0 / n**3
    f32 = jnp.float32
    dma = pltpu.SemaphoreType.DMA
    relay = phases * 2 * half
    scratch = [
        pltpu.VMEM((slab, n, n), f32),
        pltpu.VMEM((2, grids, half, n, n), f32),
        pltpu.VMEM((relay, n, n), f32),
        pltpu.VMEM((relay, n, n), f32),
        pltpu.VMEM((phases, grids, half, n, n), f32),
        pltpu.VMEM((bands, slab, yb, n), f32),
        pltpu.VMEM((slots, n * depth, n), f32),
        pltpu.VMEM((phases, n // depth, n // 2 * depth, n), f32),
        pltpu.VMEM((phases, slots, n * depth, n), f32),
        pltpu.VMEM((grids, half, n, n), f32),
        pltpu.VMEM((2, half, n, n), f32),
        pltpu.VMEM((bands, slab, yb, n), f32),
        pltpu.VMEM((bands * bands, 8, n), f32),
        pltpu.VMEM((bands, 8, n), f32),
        pltpu.VMEM((grids, 8, n), f32),
        pltpu.VMEM((n, n), f32),
        dma((3,)),
        dma((4,)), dma((4,)),
        dma((8,)), dma((8,)),
        dma((4,)), dma((4,)),
        dma((4,)), dma((4,)),
        dma((relay,)), dma((relay,)),
        dma((relay,)), dma((relay,)),
        dma((relay,)), dma((relay,)),
        dma((bands,)), dma((bands,)),
        dma((phases * slots,)), dma((phases * slots,)),
        dma((phases * slots,)), dma((phases * slots,)),
        dma((8,)), dma((8,)),
        dma((8 * bands,)), dma((8 * bands,)),
        dma((bands,)), dma((bands,)),
        dma((grids,)), dma((grids,)),
    ]
    vmem = pl.BlockSpec(memory_space=pltpu.VMEM)
    return pl.pallas_call(
        functools.partial(whole_kernel, bands, grids, rounds, 3, depth, n, volume),
        out_shape=jax.ShapeDtypeStruct((bands, slab, yb, n), f32),
        in_specs=[
            pl.BlockSpec(memory_space=pltpu.SMEM),
            pl.BlockSpec(memory_space=pl.ANY),
            vmem, vmem, vmem,
        ],
        out_specs=vmem,
        scratch_shapes=scratch,
        compiler_params=pltpu.CompilerParams(
            collective_id=0, has_side_effects=True, vmem_limit_bytes=63 * 1024 * 1024
        ),
        name="exchange",
    )(sources, orbitals, left, right, waves)


def per_device(orbitals, sources):
    held, slab, full_y, full_z = orbitals.shape
    bands = lax.axis_size("band")
    grids = lax.axis_size("grid")
    n = full_y
    rounds = sources.shape[0]
    fits = (
        held == 1 and n == full_z == slab * grids and n % 128 == 0 and slab % 32 == 0
        and grids == 4 and rounds == grids and bands % 2 == 0 and bands * bands <= n
        and n % (8 * bands) == 0 and 4 * n * n * slab * 29 <= 60 * 2**20
    )
    if fits:
        return fused(bands, grids, orbitals, sources)
    return general(orbitals, sources)


def solution(mesh):
    placed = (P("band", "grid", None, None), P())
    return jax.shard_map(
        per_device,
        mesh=mesh,
        in_specs=placed,
        out_specs=P(None, "grid", "band", None),
        check_vma=False,
    )
```

time: 244 us -> 235 us (0.963)
  Pallas kernels: 240 us -> 232 us
    pallas_call x1, Pallas kernels: 240 us -> 232 us  [fused(): pl.pallas_call(functools.partial(whole_kernel, bands, grids, rounds, 3, d...]
where the time goes in v2:
time: 235 us
  Pallas kernels  232 us (99%)
  local copies, waits for them, and re-layouts  3.05 us (1%)
    pallas_call x1, Pallas kernels, fused(): pl.pallas_call(functools.partial(whole_kernel, bands, grids, rounds, 3, d...  232 us

profile of v2, /device:TPU:0, one launch (start us, length us, event | category | flops | bytes accessed | tf_op | source)
XLA Modules:
  0.0 235.0 jit_solution(7092202321597133811)
XLA Ops:
  0.0 232.0 %exchange.1 = f32[8,32,16,128]{3,2,1,0:T(8,128)} custom-call(s32[4]{0:T(128)} %sources.1, f32[1,32,128,128]{3,2,1,0:T(8,128)} %orbitals.1, bf16[256,256]{1,0:T(8,128)(2,1)} %constant.13.left_ref, bf16[256,256]{1,0:T(8,128)(2,1)} %constant.15.right_ref, f32[128,128]{1,0:T(8,128)} %constant.5.clone.waves_ref), custom_call_target="tpu_custom_call" | custom-call | tf_op jit(solution)/shard_map/exchange/pallas_call | solution.py:727
  232.0 3.0 %copy.6 = f32[8,32,16,128]{3,2,1,0:T(8,128)} copy(f32[8,32,16,128]{3,2,1,0:T(8,128)} %exchange.1) | data formatting | bytes 4194304

commit v3 on v2

--- a/solution.py
+++ b/solution.py
@@ -127,7 +127,7 @@
 
 
 def whole_kernel(
-    bands, grids, rounds, ahead, depth, n, volume,
+    bands, grids, rounds, ahead, early, depth, n, volume,
     sources, orbitals, left_ref, right_ref, waves_ref, out, *scratch,
 ):
     (own, orb, up, dn, src, fcol, spec, cols, back, terms, pin, tcol, part, sums_b, sums_g, splat,
@@ -145,6 +145,8 @@
     pieces = half // depth
     slots = grids * pieces
     quarter = half // 4
+    pair = 2
+    pairs = half // pair
     mine = n // 2 * depth
     phases = rounds // 2
     total_units = phases * 2 * half
@@ -240,8 +242,18 @@
             device_id=(b, gy), device_id_type=MESH,
         )
 
+    def o_copy(target, owner, late):
+        planes = pl.ds(early, slab - early) if late else pl.ds(0, early)
+        return pltpu.make_async_remote_copy(
+            src_ref=own.at[planes, pl.ds(target * yb, yb)], dst_ref=fcol.at[owner, planes],
+            send_sem=o_send.at[late * bands + target], recv_sem=o_recv.at[late * bands + owner],
+            device_id=(target, g), device_id_type=MESH,
+        )
+
     for u in range(4):
         mate_copy(u, core).start()
+    for d in range(1, bands):
+        o_copy(lax.rem(b + d, bands), b, 0).start()
     for u in range(4):
         mate_copy(u, 1 - core).wait_recv()
         oy_copy(u, 1 - row, g).start()
@@ -361,7 +373,7 @@
     lines_count = n // 4
 
     def lines(q, first, count):
-        def line(k, _):
+        def line(k):
             held = [
                 cols[q, :, pl.ds(pl.multiple_of((2 * k + e) * depth, depth), depth), :].reshape(n, n)
                 for e in range(2)
@@ -378,9 +390,13 @@
                 cols[q, :, pl.ds(pl.multiple_of((2 * k + e) * depth, depth), depth), :] = (
                     done[:, e * n:(e + 1) * n].reshape(n // depth, depth, n)
                 )
+
+        def group(i, _):
+            for e in range(2):
+                line(first + 2 * i + e)
             return 0
 
-        lax.fori_loop(first, first + count, line, 0)
+        lax.fori_loop(0, count // 2, group, 0)
 
     def inverse(q, at, piece):
         slot = at * pieces + piece
@@ -401,25 +417,19 @@
             else:
                 terms[at, here] += value
 
-    def o_copy(target, owner):
-        return pltpu.make_async_remote_copy(
-            src_ref=own.at[:, pl.ds(target * yb, yb)], dst_ref=fcol.at[owner],
-            send_sem=o_send.at[target], recv_sem=o_recv.at[owner],
-            device_id=(target, g), device_id_type=MESH,
-        )
-
     def p_copy(at, side, m):
         return pltpu.make_async_remote_copy(
-            src_ref=terms.at[at, pl.ds(m * quarter, quarter)],
-            dst_ref=pin.at[side, pl.ds(m * quarter, quarter)],
-            send_sem=p_send.at[side * 4 + m], recv_sem=p_recv.at[side * 4 + m],
+            src_ref=terms.at[at, pl.ds(m * pair, pair)],
+            dst_ref=pin.at[side, pl.ds(m * pair, pair)],
+            send_sem=p_send.at[side * pairs + m], recv_sem=p_recv.at[side * pairs + m],
             device_id=(b, gx), device_id_type=MESH,
         )
 
     def bounds(q, remote):
         local = [q * 2 * half + lag + side * half + (p + 1) * depth for side in range(2) for p in range(2)]
         far = [at + remote for at in local]
-        return [local[0], local[1], far[0], local[2], far[1], local[3], far[2], far[3]]
+        last = [far[2] + 6, far[3] + 1] if q == 0 else far[2:]
+        return [local[0], local[1], far[0], local[2], far[1], local[3], *last]
 
     first_bounds = bounds(0, 10)
     second_bounds = bounds(1, 10)
@@ -456,7 +466,7 @@
         @pl.when(i == 5)
         def _():
             for d in range(1, bands):
-                o_copy(lax.rem(b + d, bands), b).start()
+                o_copy(lax.rem(b + d, bands), b, 1).start()
 
         return stop
 
@@ -475,8 +485,8 @@
 
         @pl.when(i < 2 * pieces)
         def _():
-            for e in range(2):
-                p_copy(at, lax.div(i, pieces), 2 * piece + e).start()
+            for e in range(depth // pair):
+                p_copy(at, lax.div(i, pieces), depth // pair * piece + e).start()
 
         return 0
 
@@ -484,31 +494,32 @@
 
     orbital = 2 * z + row
 
+    wait = 3
     def t_copy(m, at, target):
-        rows = pl.ds(m * quarter, quarter)
+        rows = pl.ds(m * pair, pair)
         return pltpu.make_async_remote_copy(
             src_ref=terms.at[at, rows, pl.ds(target * yb, yb)],
-            dst_ref=tcol.at[orbital, pl.ds(core * half + m * quarter, quarter)],
-            send_sem=t_send.at[(jnp.where(at == g, 1, 0) * 4 + m) * bands + target],
-            recv_sem=t_recv.at[(orbital * 2 + core) * 4 + m],
+            dst_ref=tcol.at[orbital, pl.ds(core * half + m * pair, pair)],
+            send_sem=t_send.at[(jnp.where(at == g, 1, 0) * pairs + m) * bands + target],
+            recv_sem=t_recv.at[(orbital * 2 + core) * pairs + m],
             device_id=(target, at), device_id_type=MESH,
         )
 
     def t_arrival(m, which, side):
-        block = tcol.at[which, pl.ds(side * half + m * quarter, quarter)]
+        block = tcol.at[which, pl.ds(side * half + m * pair, pair)]
         return pltpu.make_async_remote_copy(
             src_ref=block, dst_ref=block,
-            send_sem=t_send.at[0], recv_sem=t_recv.at[(which * 2 + side) * 4 + m],
+            send_sem=t_send.at[0], recv_sem=t_recv.at[(which * 2 + side) * pairs + m],
             device_id=(partner, g), device_id_type=MESH,
         )
 
     def finish(i, _):
-        @pl.when(i < 8)
-        def _():
-            own_side = lax.div(i, 4)
-            m = lax.rem(i, 4)
+        @pl.when(i < 2 * pairs)
+        def _():
+            own_side = lax.div(i, pairs)
+            m = lax.rem(i, pairs)
             at = jnp.where(own_side == 0, gy, g)
-            rows = pl.ds(m * quarter, quarter)
+            rows = pl.ds(m * pair, pair)
             p_copy(at, own_side, m).wait_recv()
             terms[at, rows] += pin[own_side, rows]
 
@@ -521,19 +532,20 @@
             def _():
                 for d in range(1, bands):
                     t_copy(m, g, lax.rem(b + d, bands)).start()
-                tcol[orbital, pl.ds(core * half + m * quarter, quarter)] = terms[
+                tcol[orbital, pl.ds(core * half + m * pair, pair)] = terms[
                     g, rows, pl.ds(b * yb, yb), :
                 ]
 
-        @pl.when(i == 2)
+        @pl.when(i == wait)
         def _():
             for d in range(1, bands):
-                o_copy(b, lax.rem(b + d, bands)).wait_recv()
-
-        @pl.when(i >= 2)
-        def _():
-            own_side = lax.div(i - 2, 4)
-            m = lax.rem(i - 2, 4)
+                for late in range(2):
+                    o_copy(b, lax.rem(b + d, bands), late).wait_recv()
+
+        @pl.when(i >= wait)
+        def _():
+            own_side = lax.div(i - wait, pairs)
+            m = lax.rem(i - wait, pairs)
             parity = jnp.where(own_side == 0, 1 - row, row)
             for k in range(nz):
                 for side in range(2):
@@ -546,12 +558,12 @@
                         t_arrival(m, 2 * k + parity, side).wait_recv()
 
             def one(a, _):
-                held = [fcol[a, pl.ds(side * half + m * quarter, quarter)] for side in range(2)]
+                held = [fcol[a, pl.ds(side * half + m * pair, pair)] for side in range(2)]
                 for k in range(nz):
                     which = 2 * k + parity
                     total = jnp.zeros((8, n), jnp.float32)
                     for side in range(2):
-                        prod = held[side] * tcol[which, pl.ds(side * half + m * quarter, quarter)]
+                        prod = held[side] * tcol[which, pl.ds(side * half + m * pair, pair)]
                         total = total + jnp.sum(prod.reshape(-1, 8, n), axis=0)
                     part[a * bands + which] += total
                 return 0
@@ -560,7 +572,7 @@
 
         return 0
 
-    lax.fori_loop(0, 10, finish, 0)
+    lax.fori_loop(0, 2 * pairs + wait, finish, 0)
 
     count = bands * bands
     flat = jnp.sum(part[...], axis=1)
@@ -653,7 +665,7 @@
     every(phases - 1, lambda q, at, piece: f_copy(q, at, piece, core).wait_send())
     for q in range(phases):
         every(q, lambda q, at, piece: b_copy(q, at, piece, core).wait_send())
-    for m in range(4):
+    for m in range(pairs):
         p_copy(gd, 0, m).wait_send()
         p_copy(gx, 1, m).wait_send()
         for target in range(bands):
@@ -661,7 +673,8 @@
         for d in range(1, bands):
             t_copy(m, g, lax.rem(b + d, bands)).wait_send()
     for d in range(1, bands):
-        o_copy(lax.rem(b + d, bands), b).wait_send()
+        for late in range(2):
+            o_copy(lax.rem(b + d, bands), b, late).wait_send()
         sb_copy(lax.rem(b + d, bands), b).wait_send()
     for d in range(1, grids):
         sg_copy(lax.rem(g + d, grids), g).wait_send()
@@ -715,17 +728,17 @@
         dma((relay,)), dma((relay,)),
         dma((relay,)), dma((relay,)),
         dma((relay,)), dma((relay,)),
-        dma((bands,)), dma((bands,)),
+        dma((2 * bands,)), dma((2 * bands,)),
         dma((phases * slots,)), dma((phases * slots,)),
         dma((phases * slots,)), dma((phases * slots,)),
-        dma((8,)), dma((8,)),
-        dma((8 * bands,)), dma((8 * bands,)),
+        dma((half,)), dma((half,)),
+        dma((half * bands,)), dma((half * bands,)),
         dma((bands,)), dma((bands,)),
         dma((grids,)), dma((grids,)),
     ]
     vmem = pl.BlockSpec(memory_space=pltpu.VMEM)
     return pl.pallas_call(
-        functools.partial(whole_kernel, bands, grids, rounds, 3, depth, n, volume),
+        functools.partial(whole_kernel, bands, grids, rounds, 3, 6, depth, n, volume),
         out_shape=jax.ShapeDtypeStruct((bands, slab, yb, n), f32),
         in_specs=[
             pl.BlockSpec(memory_space=pltpu.SMEM),

time: 235 us -> 223 us (0.949)
  Pallas kernels: 232 us -> 220 us
    pallas_call x1, Pallas kernels: 232 us -> 220 us  [fused(): pl.pallas_call(functools.partial(whole_kernel, bands, grids, rounds, 3, 6...]
where the time goes in v3:
time: 223 us
  Pallas kernels  220 us (99%)
  local copies, waits for them, and re-layouts  3.05 us (1%)
    pallas_call x1, Pallas kernels, fused(): pl.pallas_call(functools.partial(whole_kernel, bands, grids, rounds, 3, 6...  220 us

profile of v3, /device:TPU:0, one launch (start us, length us, event | category | flops | bytes accessed | tf_op | source)
XLA Modules:
  0.0 223.3 jit_solution(17363663938115546453)
XLA Ops:
  0.0 220.2 %exchange.1 = f32[8,32,16,128]{3,2,1,0:T(8,128)} custom-call(s32[4]{0:T(128)} %sources.1, f32[1,32,128,128]{3,2,1,0:T(8,128)} %orbitals.1, bf16[256,256]{1,0:T(8,128)(2,1)} %constant.13.left_ref, bf16[256,256]{1,0:T(8,128)(2,1)} %constant.15.right_ref, f32[128,128]{1,0:T(8,128)} %constant.5.clone.waves_ref), custom_call_target="tpu_custom_call" | custom-call | tf_op jit(solution)/shard_map/exchange/pallas_call | solution.py:740
  220.2 3.0 %copy.6 = f32[8,32,16,128]{3,2,1,0:T(8,128)} copy(f32[8,32,16,128]{3,2,1,0:T(8,128)} %exchange.1) | data formatting | bytes 4194304

commit v4 on v3

--- a/solution.py
+++ b/solution.py
@@ -458,9 +458,11 @@
     reached = settle + slots
 
     def second_forward(i, at):
-        stop = jnp.maximum(pick(i, second_bounds), at)
-        advance(at, stop)
+        stop = jnp.maximum(pick(i, second_bounds), reached + 2 * (i + 1))
+        middle = jnp.minimum(at + 1, stop)
+        advance(at, middle)
         inverse(0, lax.div(i, pieces), lax.rem(i, pieces))
+        advance(middle, stop)
         forward(1, i)
 
         @pl.when(i == 5)
@@ -473,7 +475,9 @@
     lax.fori_loop(0, slots, second_forward, reached)
     every(1, lambda q, at, piece: f_copy(q, at, piece, 1 - core).wait_recv())
     lines(1, 0, lines_count)
-    every(1, lambda q, at, piece: b_copy(q, at, piece, core).start())
+    for at in (gd, gx, gy, g):
+        for piece in range(pieces):
+            b_copy(1, at, piece, core).start()
 
     fcol[b] = own[:, pl.ds(b * yb, yb), :]
     part[...] = jnp.zeros_like(part)

time: 223 us -> 220 us (0.987)
  Pallas kernels: 220 us -> 217 us
    pallas_call x1, Pallas kernels: 220 us -> 217 us  [fused(): pl.pallas_call(functools.partial(whole_kernel, bands, grids, rounds, 3, 6...]
where the time goes in v4:
time: 220 us
  Pallas kernels  217 us (99%)
  local copies, waits for them, and re-layouts  3.05 us (1%)
    pallas_call x1, Pallas kernels, fused(): pl.pallas_call(functools.partial(whole_kernel, bands, grids, rounds, 3, 6...  217 us

profile of v4, /device:TPU:0, one launch (start us, length us, event | category | flops | bytes accessed | tf_op | source)
XLA Modules:
  0.0 220.0 jit_solution(1098948475495543081)
XLA Ops:
  0.0 216.9 %exchange.1 = f32[8,32,16,128]{3,2,1,0:T(8,128)} custom-call(s32[4]{0:T(128)} %sources.1, f32[1,32,128,128]{3,2,1,0:T(8,128)} %orbitals.1, bf16[256,256]{1,0:T(8,128)(2,1)} %constant.13.left_ref, bf16[256,256]{1,0:T(8,128)(2,1)} %constant.15.right_ref, f32[128,128]{1,0:T(8,128)} %constant.5.clone.waves_ref), custom_call_target="tpu_custom_call" | custom-call | tf_op jit(solution)/shard_map/exchange/pallas_call | solution.py:744
  216.9 3.0 %copy.6 = f32[8,32,16,128]{3,2,1,0:T(8,128)} copy(f32[8,32,16,128]{3,2,1,0:T(8,128)} %exchange.1) | data formatting | bytes 4194304

commit v5 on v4

--- a/solution.py
+++ b/solution.py
@@ -130,11 +130,11 @@
     bands, grids, rounds, ahead, early, depth, n, volume,
     sources, orbitals, left_ref, right_ref, waves_ref, out, *scratch,
 ):
-    (own, orb, up, dn, src, fcol, spec, cols, back, terms, pin, tcol, part, sums_b, sums_g, splat,
+    (own, orb, up, dn, src, fcol, spec, cols, back, terms, pin, tcol, held_out, part, sums_b, sums_g, splat,
      in_sem, m_send, m_recv, ox_send, ox_recv, oy_send, oy_recv, or_send, or_recv,
      up_send, up_recv, dn_send, dn_recv, y_send, y_recv, o_send, o_recv, f_send, f_recv,
      b_send, b_recv, p_send, p_recv, t_send, t_recv,
-     sb_send, sb_recv, sg_send, sg_recv) = scratch
+     sb_send, sb_recv, sg_send, sg_recv, out_sem) = scratch
     b = lax.axis_index("band")
     g = lax.axis_index("grid")
     nz = bands // 2
@@ -465,10 +465,13 @@
         advance(middle, stop)
         forward(1, i)
 
-        @pl.when(i == 5)
-        def _():
-            for d in range(1, bands):
-                o_copy(lax.rem(b + d, bands), b, 1).start()
+        for d in range(1, bands):
+            target = lax.rem(b + d, bands)
+            nearer = lax.div(target, 2) == jnp.where(z < nz // 2, nz // 2, nz // 2 - 1)
+
+            @pl.when(i == jnp.where(nearer, 4, 5))
+            def _():
+                o_copy(target, b, 1).start()
 
         return stop
 
@@ -632,6 +635,10 @@
         for i in range(k + 1, bands):
             splat[pl.ds(i * bands + k, 1), :] = factor[i, k]
 
+    def leave(p):
+        x = pl.ds(4 * p, 4)
+        return pltpu.make_async_copy(held_out.at[:, x], out.at[:, x], out_sem.at[p])
+
     def solve(p, _):
         x = pl.ds(4 * p, 4)
         solved = []
@@ -640,12 +647,15 @@
             for k in range(i):
                 value = value - splat[pl.ds(i * bands + k, 1), :] * solved[k]
             value = value * splat[pl.ds(i * bands + i, 1), :]
-            out[i, x] = value
+            held_out[i, x] = value
             solved.append(value)
+        leave(p).start()
         return 0
 
     lax.fori_loop(0, slab // 4, solve, 0)
 
+    for p in range(slab // 4):
+        leave(p).wait()
     for u in range(4):
         mate_copy(u, core).wait_send()
         oy_copy(u, 1 - row, g).wait_send()
@@ -720,6 +730,7 @@
         pltpu.VMEM((grids, half, n, n), f32),
         pltpu.VMEM((2, half, n, n), f32),
         pltpu.VMEM((bands, slab, yb, n), f32),
+        pltpu.VMEM((bands, slab, yb, n), f32),
         pltpu.VMEM((bands * bands, 8, n), f32),
         pltpu.VMEM((bands, 8, n), f32),
         pltpu.VMEM((grids, 8, n), f32),
@@ -739,17 +750,18 @@
         dma((half * bands,)), dma((half * bands,)),
         dma((bands,)), dma((bands,)),
         dma((grids,)), dma((grids,)),
+        dma((slab // 4,)),
     ]
     vmem = pl.BlockSpec(memory_space=pltpu.VMEM)
     return pl.pallas_call(
-        functools.partial(whole_kernel, bands, grids, rounds, 3, 6, depth, n, volume),
+        functools.partial(whole_kernel, bands, grids, rounds, 3, slab // 2, depth, n, volume),
         out_shape=jax.ShapeDtypeStruct((bands, slab, yb, n), f32),
         in_specs=[
             pl.BlockSpec(memory_space=pltpu.SMEM),
             pl.BlockSpec(memory_space=pl.ANY),
             vmem, vmem, vmem,
         ],
-        out_specs=vmem,
+        out_specs=pl.BlockSpec(memory_space=pl.ANY),
         scratch_shapes=scratch,
         compiler_params=pltpu.CompilerParams(
             collective_id=0, has_side_effects=True, vmem_limit_bytes=63 * 1024 * 1024

time: 220 us -> 212 us (0.964)
  Pallas kernels: 217 us -> 209 us
    pallas_call x1, Pallas kernels: 217 us -> 209 us  [fused(): pl.pallas_call(functools.partial(whole_kernel, bands, grids, rounds, 3, s...]
where the time goes in v5:
time: 212 us
  Pallas kernels  209 us (99%)
  local copies, waits for them, and re-layouts  3.05 us (1%)
    pallas_call x1, Pallas kernels, fused(): pl.pallas_call(functools.partial(whole_kernel, bands, grids, rounds, 3, s...  209 us

profile of v5, /device:TPU:0, one launch (start us, length us, event | category | flops | bytes accessed | tf_op | source)
XLA Modules:
  0.0 212.2 jit_solution(17882664016554400380)
XLA Ops:
  0.0 209.2 %exchange.1 = f32[8,32,16,128]{3,2,1,0:T(8,128)} custom-call(s32[4]{0:T(128)} %sources.1, f32[1,32,128,128]{3,2,1,0:T(8,128)} %orbitals.1, bf16[256,256]{1,0:T(8,128)(2,1)} %constant.13.left_ref, bf16[256,256]{1,0:T(8,128)(2,1)} %constant.15.right_ref, f32[128,128]{1,0:T(8,128)} %constant.5.clone.waves_ref), custom_call_target="tpu_custom_call" | custom-call | tf_op jit(solution)/shard_map/exchange/pallas_call | solution.py:756
  209.2 3.0 %copy.6 = f32[8,32,16,128]{3,2,1,0:T(8,128)} copy(f32[8,32,16,128]{3,2,1,0:T(8,128)} %exchange.1) | data formatting | bytes 4194304

commit v6 on v5

--- a/solution.py
+++ b/solution.py
@@ -532,8 +532,8 @@
 
             @pl.when(own_side == 0)
             def _():
-                for target in range(bands):
-                    t_copy(m, gy, target).start()
+                for d in range(bands):
+                    t_copy(m, gy, lax.rem(b + d, bands)).start()
 
             @pl.when(own_side == 1)
             def _():

time: 212 us -> 212 us (level)
  no operation moved by 1% of the time
where the time goes in v6:
time: 212 us
  Pallas kernels  209 us (99%)
  local copies, waits for them, and re-layouts  3.05 us (1%)
    pallas_call x1, Pallas kernels, fused(): pl.pallas_call(functools.partial(whole_kernel, bands, grids, rounds, 3, s...  209 us

profile of v6, /device:TPU:0, one launch (start us, length us, event | category | flops | bytes accessed | tf_op | source)
XLA Modules:
  0.0 212.2 jit_solution(13381714104318471749)
XLA Ops:
  0.0 209.2 %exchange.1 = f32[8,32,16,128]{3,2,1,0:T(8,128)} custom-call(s32[4]{0:T(128)} %sources.1, f32[1,32,128,128]{3,2,1,0:T(8,128)} %orbitals.1, bf16[256,256]{1,0:T(8,128)(2,1)} %constant.13.left_ref, bf16[256,256]{1,0:T(8,128)(2,1)} %constant.15.right_ref, f32[128,128]{1,0:T(8,128)} %constant.5.clone.waves_ref), custom_call_target="tpu_custom_call" | custom-call | tf_op jit(solution)/shard_map/exchange/pallas_call | solution.py:756
  209.2 3.0 %copy.6 = f32[8,32,16,128]{3,2,1,0:T(8,128)} copy(f32[8,32,16,128]{3,2,1,0:T(8,128)} %exchange.1) | data formatting | bytes 4194304
